TPU v7x, 32 devices: a whole 2x2x4 slice. The times are simulated.
32 devices in a mesh: cuts: 2 (over x), mode: 16 (over z, y, core).
Axes of the slice: x: 2, y: 2, z: 4, core: 2. Of those that a mesh axis runs over, the one named last changes fastest.
Arguments:
- stem_tensor: float32 [2, 2, 16, 512, 512], P(None, 'cuts', 'mode'), parts along dimension 1, may hold values from -6 to 6
- branch_tensors: float32 [4, 2, 512, 512], replicated, may hold values from -0.1875 to 0.1875
- branch_order: int32 [4], replicated, may hold values from 0 to 3, each once
Outputs:
- new_stem: float32 [2, 2, 16, 512, 512], P(None, 'cuts', 'mode'), parts along dimension 1
There are 2 independent parts, one for each index of `cuts`. A program takes and returns all parts, laid end to end along the dimension named above; an argument that names none is the same for every part. Nothing has to cross between parts.
Inputs may be any that keep to these rules, and one draw needn't show every extreme that they name: `branch_order`: a permutation of the 4 branch tensors.
All inputs are finite; a program needn't handle non-finite values.
Results may differ from a plain program's by a relative error of at most 0.00007.
Values sent between devices are 32-bit elements; how exact they have to be, the bound alone decides.
A program may use at most 64 MiB of HBM per device.

v0:
```python
import jax
import jax.numpy as jnp
from jax import lax
from jax.sharding import PartitionSpec as P


def complex_product(first, second, form):
    high = lax.Precision.HIGHEST
    real = jnp.einsum(form, first[0], second[0], precision=high) - jnp.einsum(
        form, first[1], second[1], precision=high
    )
    imag = jnp.einsum(form, first[0], second[1], precision=high) + jnp.einsum(
        form, first[1], second[0], precision=high
    )
    return jnp.stack([real, imag])


def on_device(stem_tensor, branch_tensors, branch_order):
    field = stem_tensor[:, :, 0]
    chosen = [branch_tensors[branch_order[index]] for index in range(4)]
    field = complex_product(field, chosen[0], "sce,cd->sde")
    field = complex_product(field, chosen[1], "sce,ed->scd")
    moved = lax.all_to_all(field[:, :, None], "mode", split_axis=3, concat_axis=2, tiled=True)
    merged = moved.reshape(field.shape)
    merged = complex_product(merged, chosen[2], "sce,cd->sde")
    return complex_product(merged, chosen[3], "sce,ed->scd")[:, :, None]


def solution(mesh):
    return jax.shard_map(
        on_device,
        mesh=mesh,
        in_specs=(P(None, "cuts", "mode", None, None), P(), P()),
        out_specs=P(None, "cuts", "mode", None, None),
        check_vma=False,
    )
```

profile of v0, /device:TPU:9, one launch (start us, length us, event | category | flops | bytes accessed | tf_op | source)
XLA Modules:
  0.0 111.7 jit_solution(4636353543271433322)
XLA Ops:
  0.0 1.5 %fusion.45 = (s32[1]{0:T(128)}, s32[1]{0:T(128)}, s32[1]{0:T(128)}, s32[1]{0:T(128)}) fusion(s32[4]{0:T(128)} %param.5), kind=kLoop, calls=%fused_computation.63 | loop fusion | bytes 32 | tf_op jit(solution)/shard_map/slice | solution.py:20
  4.7 0.0 copy-start
  4.7 3.5 %fusion.14 = f32[512,512]{1,0:T(8,128)S(1)} fusion(f32[2,1,1,512,512]{4,3,2,1,0:T(8,128)} %param.3, f32[4,2,512,512]{3,2,1,0:T(8,128)} %param.4, s32[]{:T(128)S(6)} %select_n.13), kind=kOutput, calls=%fused_computation.32 | convolution fusion | flops 1610612736 | bytes 3145732 | tf_op jit(solution)/shard_map/sce,cd->sde/dot_general | solution.py:9
  8.2 4.4 %fusion.12 = f32[512,512]{1,0:T(8,128)} fusion(f32[2,1,1,512,512]{4,3,2,1,0:T(8,128)} %param.3, f32[4,2,512,512]{3,2,1,0:T(8,128)} %param.4, s32[]{:T(128)S(6)} %select_n.13, s32[]{:T(128)S(6)} %add.36), kind=kOutput, calls=%fused_computation.30 | convolution fusion | flops 1610612736 | bytes 3145736 | tf_op jit(solution)/shard_map/sce,cd->sde/dot_general | solution.py:12
  12.6 3.4 %convolution_subtract_fusion.3 = f32[512,512]{1,0:T(8,128)S(1)} fusion(f32[512,512]{1,0:T(8,128)S(1)} %fusion.14, f32[2,1,1,512,512]{4,3,2,1,0:T(8,128)} %param.3, f32[4,2,512,512]{3,2,1,0:T(8,128)} %param.4, s32[]{:T(128)S(6)} %select_n.13, s32[]{:T(128)S(6)} %add.36), kind=kOutput, calls=%fused_computation.13 | convolution fusion | flops 1610874880 | bytes 4194312 | tf_op jit(solution)/shard_map/sce,cd->sde/dot_general | solution.py:9
  16.6 3.1 %fusion.26 = f32[512,512]{1,0:T(8,128)S(1)} fusion(f32[512,512]{1,0:T(8,128)S(1)} %convolution_subtract_fusion.3, f32[4,2,512,512]{3,2,1,0:T(8,128)} %param.4, s32[]{:T(128)S(6)} %select_n.14, s32[]{:T(128)S(6)} %add.36), kind=kOutput, calls=%fused_computation.44 | convolution fusion | flops 1610612736 | bytes 3145736 | tf_op jit(solution)/shard_map/sce,ed->scd/dot_general | solution.py:12
  19.7 3.1 %fusion.24 = f32[512,512]{1,0:T(8,128)S(1)} fusion(f32[512,512]{1,0:T(8,128)S(1)} %convolution_subtract_fusion.3, f32[4,2,512,512]{3,2,1,0:T(8,128)} %param.4, s32[]{:T(128)S(6)} %select_n.14), kind=kOutput, calls=%fused_computation.42 | convolution fusion | flops 1610612736 | bytes 3145732 | tf_op jit(solution)/shard_map/sce,ed->scd/dot_general | solution.py:9
  22.8 0.0 copy-done
  22.8 3.4 %convolution_add_fusion.3 = f32[512,512]{1,0:T(8,128)S(1)} fusion(f32[512,512]{1,0:T(8,128)} %fusion.12, f32[2,1,1,512,512]{4,3,2,1,0:T(8,128)S(1)} %copy-done, f32[4,2,512,512]{3,2,1,0:T(8,128)} %param.4, s32[]{:T(128)S(6)} %select_n.13), kind=kOutput, calls=%fused_computation.12 | convolution fusion | flops 1610874880 | bytes 4194308 | tf_op jit(solution)/shard_map/sce,cd->sde/dot_general | solution.py:12
  26.2 3.3 %fusion.3 = f32[1,1,512,512]{3,2,1,0:T(8,128)S(1)} fusion(f32[512,512]{1,0:T(8,128)S(1)} %fusion.24, f32[512,512]{1,0:T(8,128)S(1)} %convolution_add_fusion.3, f32[4,2,512,512]{3,2,1,0:T(8,128)} %param.4, s32[]{:T(128)S(6)} %select_n.14, s32[]{:T(128)S(6)} %add.36), kind=kOutput, calls=%fused_computation.11 | convolution fusion | flops 1610874880 | bytes 4194312 | tf_op jit(solution)/shard_map/sce,ed->scd/dot_general | solution.py:9
  29.5 3.1 %fusion.2 = f32[1,1,512,512]{3,2,1,0:T(8,128)S(1)} fusion(f32[512,512]{1,0:T(8,128)S(1)} %fusion.26, f32[512,512]{1,0:T(8,128)S(1)} %convolution_add_fusion.3, f32[4,2,512,512]{3,2,1,0:T(8,128)} %param.4, s32[]{:T(128)S(6)} %select_n.14), kind=kOutput, calls=%fused_computation.9 | convolution fusion | flops 1610874880 | bytes 4194308 | tf_op jit(solution)/shard_map/sce,ed->scd/dot_general | solution.py:12
  32.6 0.2 maximum_bitcast_fusion
  32.7 2.9 %copy.5 = f32[2,1,1,512,512]{4,0,2,1,3:T(2,128)} copy(f32[2,1,1,512,512]{4,3,0,2,1:T(8,128)S(1)} %maximum_bitcast_fusion) | data formatting | bytes 4194304 | tf_op jit(solution)/shard_map/broadcast_in_dim | solution.py:23
  35.7 6.6 %all-to-all-start = ((f32[2,1,1,512,512]{4,0,2,1,3:T(2,128)}), f32[2,1,1,512,512]{4,0,2,1,3:T(2,128)S(1)}, u32[]{:S(2)}, u32[]{:S(2)}) async-start(f32[2,1,1,512,512]{4,0,2,1,3:T(2,128)} %copy.5), calls=%async_computation | async-start | bytes 4194304 | tf_op jit(solution)/shard_map/all_to_all | solution.py:23
  46.2 42.2 %all-to-all-done = f32[2,1,1,512,512]{4,0,2,1,3:T(2,128)S(1)} async-done(((f32[2,1,1,512,512]{4,0,2,1,3:T(2,128)}), f32[2,1,1,512,512]{4,0,2,1,3:T(2,128)S(1)}, u32[]{:S(2)}, u32[]{:S(2)}) %all-to-all-start) | async-done | bytes 2097184 | tf_op jit(solution)/shard_map/all_to_all | solution.py:23
  88.3 0.0 slice-start
  88.3 1.6 %fusion.44 = (f32[1,1,1,512,512]{4,0,2,1,3:T(1,128)S(1)}, f32[1,1,1,512,512]{4,0,2,1,3:T(1,128)S(1)}) fusion(f32[2,1,1,512,512]{4,0,2,1,3:T(2,128)S(1)} %all-to-all-done), kind=kLoop, calls=%fused_computation.62 | loop fusion | bytes 4194304 | tf_op jit(solution)/shard_map/slice | solution.py:10
  90.0 3.1 %fusion.6 = f32[512,512]{1,0:T(8,128)S(1)} fusion(f32[1,1,1,512,512]{4,0,2,1,3:T(1,128)S(1)} %get-tuple-element.6, f32[4,2,512,512]{3,2,1,0:T(8,128)} %param.4, s32[]{:T(128)S(6)} %select_n.12, s32[]{:T(128)S(6)} %add.36), kind=kOutput, calls=%fused_computation.24 | convolution fusion | flops 1610612736 | bytes 3145736 | tf_op jit(solution)/shard_map/sce,cd->sde/dot_general | solution.py:12
  93.0 0.0 slice-start.1
  93.1 3.2 %fusion.8 = f32[512,512]{1,0:T(8,128)S(1)} fusion(f32[1,1,1,512,512]{4,0,2,1,3:T(1,128)S(1)} %get-tuple-element.6, f32[4,2,512,512]{3,2,1,0:T(8,128)} %param.4, s32[]{:T(128)S(6)} %select_n.12), kind=kOutput, calls=%fused_computation.26 | convolution fusion | flops 1610612736 | bytes 3145732 | tf_op jit(solution)/shard_map/sce,cd->sde/dot_general | solution.py:9
  96.3 3.1 %convolution_subtract_fusion.1 = f32[512,512]{1,0:T(8,128)S(1)} fusion(f32[512,512]{1,0:T(8,128)S(1)} %fusion.8, f32[1,1,1,512,512]{4,0,2,1,3:T(1,128)S(1)} %get-tuple-element.5, f32[4,2,512,512]{3,2,1,0:T(8,128)} %param.4, s32[]{:T(128)S(6)} %select_n.12, s32[]{:T(128)S(6)} %add.36), kind=kOutput, calls=%fused_computation.7 | convolution fusion | flops 1610874880 | bytes 4194312 | tf_op jit(solution)/shard_map/sce,cd->sde/dot_general | solution.py:9
  99.4 3.1 %fusion.27 = f32[512,512]{1,0:T(8,128)S(1)} fusion(f32[512,512]{1,0:T(8,128)S(1)} %convolution_subtract_fusion.1, f32[4,2,512,512]{3,2,1,0:T(8,128)} %param.4, s32[]{:T(128)S(6)} %select_n.15, s32[]{:T(128)S(6)} %add.36), kind=kOutput, calls=%fused_computation.45 | convolution fusion | flops 1610612736 | bytes 3145736 | tf_op jit(solution)/shard_map/sce,ed->scd/dot_general | solution.py:12
  102.5 0.0 slice-done
  102.5 0.0 slice-done.1
  102.5 1.8 %fusion.25 = f32[512,512]{1,0:T(8,128)S(1)} fusion(f32[512,512]{1,0:T(8,128)S(1)} %convolution_subtract_fusion.1, f32[4,2,512,512]{3,2,1,0:T(8,128)S(1)} %bitcast.79, s32[]{:T(128)S(6)} %select_n.15), kind=kOutput, calls=%fused_computation.43 | convolution fusion | flops 1610612736 | bytes 3145732 | tf_op jit(solution)/shard_map/sce,ed->scd/dot_general | solution.py:9
  104.4 2.2 %convolution_add_fusion.1 = f32[512,512]{1,0:T(8,128)S(1)} fusion(f32[512,512]{1,0:T(8,128)S(1)} %fusion.6, f32[1,1,1,512,512]{4,0,2,1,3:T(1,128)S(1)} %get-tuple-element.5, f32[4,2,512,512]{3,2,1,0:T(8,128)S(1)} %bitcast.79, s32[]{:T(128)S(6)} %select_n.12), kind=kOutput, calls=%fused_computation.6 | convolution fusion | flops 1610874880 | bytes 4194308 | tf_op jit(solution)/shard_map/sce,cd->sde/dot_general | solution.py:12
  106.5 1.8 %fusion.1 = f32[1,1,512,512]{3,2,1,0:T(8,128)S(1)} fusion(f32[512,512]{1,0:T(8,128)S(1)} %fusion.25, f32[512,512]{1,0:T(8,128)S(1)} %convolution_add_fusion.1, f32[4,2,512,512]{3,2,1,0:T(8,128)S(1)} %bitcast.79, s32[]{:T(128)S(6)} %select_n.15, s32[]{:T(128)S(6)} %add.36), kind=kOutput, calls=%fused_computation.5 | convolution fusion | flops 1610874880 | bytes 4194312 | tf_op jit(solution)/shard_map/sce,ed->scd/dot_general | solution.py:9
  108.4 1.8 %fusion = f32[1,1,512,512]{3,2,1,0:T(8,128)S(1)} fusion(f32[512,512]{1,0:T(8,128)S(1)} %fusion.27, f32[512,512]{1,0:T(8,128)S(1)} %convolution_add_fusion.1, f32[4,2,512,512]{3,2,1,0:T(8,128)S(1)} %bitcast.79, s32[]{:T(128)S(6)} %select_n.15), kind=kOutput, calls=%fused_computation.3 | convolution fusion | flops 1610874880 | bytes 4194308 | tf_op jit(solution)/shard_map/sce,ed->scd/dot_general | solution.py:12
  110.2 1.5 %maximum_bitcast_fusion.1 = f32[2,1,1,512,512]{4,3,2,1,0:T(8,128)} fusion(f32[1,1,512,512]{3,2,1,0:T(8,128)S(1)} %fusion, f32[1,1,512,512]{3,2,1,0:T(8,128)S(1)} %fusion.1), kind=kLoop, calls=%fused_computation.1 | loop fusion | flops 524288 | bytes 4194304 | tf_op jit(solution)/shard_map/broadcast_in_dim | solution.py:26
  (1 shorter events, 0.0 us)
Async XLA Ops:
  4.7 18.1 %copy-start = (f32[2,1,1,512,512]{4,3,2,1,0:T(8,128)S(1)}, f32[2,1,1,512,512]{4,3,2,1,0:T(8,128)}, u32[]{:S(2)}) copy-start(f32[2,1,1,512,512]{4,3,2,1,0:T(8,128)} %param.3) | copy-start | bytes 6291460
  35.7 52.7 %all-to-all-start = ((f32[2,1,1,512,512]{4,0,2,1,3:T(2,128)}), f32[2,1,1,512,512]{4,0,2,1,3:T(2,128)S(1)}, u32[]{:S(2)}, u32[]{:S(2)}) async-start(f32[2,1,1,512,512]{4,0,2,1,3:T(2,128)} %copy.5), calls=%async_computation | async-start | bytes 4194304 | tf_op jit(solution)/shard_map/all_to_all | solution.py:23
  88.3 14.2 %slice-start = ((s8[8388608]{0:T(1024)(128)(4,1)}), s8[4194304]{0:T(1024)(128)(4,1)S(1)}, s32[]{:S(2)}) async-start(s8[8388608]{0:T(1024)(128)(4,1)} %bitcast.78), calls=%async_computation.1 | async-start | bytes 8388608
  93.0 9.5 %slice-start.1 = ((s8[8388608]{0:T(1024)(128)(4,1)}), s8[4194304]{0:T(1024)(128)(4,1)S(1)}, s32[]{:S(2)}) async-start(s8[8388608]{0:T(1024)(128)(4,1)} %bitcast.78), calls=%async_computation.2 | async-start | bytes 8388608
where the time goes:
time: 114 us; the launch traced here: 112 us
  matrix products  47.4 us (42%)
  waiting for transfers between devices  42.2 us (37%)
  between operations  7.96 us (7%)
  starting transfers between devices  6.58 us (6%)
  local copies, waits for them, and re-layouts  6.03 us (5%)
  other arithmetic  1.66 us (1%)
    all_to_all x1, waiting for transfers between devices, on_device(): lax.all_to_all(field[:, :, None], 'mode', split_axis=3, concat_axis=2, ti...  42.2 us
    dot_general x4, matrix products, complex_product(): jnp.einsum(form, first[0], second[1], precision=high)  13.6 us
    dot_general x4, matrix products, complex_product(): jnp.einsum(form, first[0], second[0], precision=high)  11.7 us
    dot_general x4, matrix products, complex_product(): jnp.einsum(form, first[1], second[1], precision=high)  11.6 us
    dot_general x4, matrix products, complex_product(): jnp.einsum(form, first[1], second[0], precision=high)  10.5 us
    all_to_all x1, starting transfers between devices, on_device(): lax.all_to_all(field[:, :, None], 'mode', split_axis=3, concat_axis=2, ti...  6.58 us
    broadcast_in_dim x1, local copies, waits for them, and re-layouts, on_device(): field[:, :, None]  2.94 us
  transfers between devices with their start and end apart: 1, of which 1 were waited for; matrix products, arithmetic and copies ran while one was open for 0% of the time, Pallas kernels for 0%

commit v1 on v0

v1 whole, which is shorter than its diff:
```python
import functools

import jax
import jax.numpy as jnp
from jax import lax
from jax.experimental import pallas as pl
from jax.experimental.pallas import tpu as pltpu
from jax.sharding import PartitionSpec as P

MESH = pl.DeviceIdType.MESH
LANES = 128
F32, BF16 = jnp.float32, jnp.bfloat16


def flip(value, mask, size):
    result, bit = 0, 1
    while bit < size:
        digit = lax.rem(lax.div(value, bit), 2)
        result = result + (1 - digit if (mask // bit) % 2 else digit) * bit
        bit *= 2
    return result


def split(value):
    high = value.astype(BF16)
    return high, (value - high.astype(F32)).astype(BF16)


def dot(a, b):
    return jnp.dot(a, b, preferred_element_type=F32)


def dot3(high, low, right_high, right_low):
    return dot(high, right_high) + (dot(high, right_low) + dot(low, right_high))


def complex_rows(rows, right_high, right_low):
    m = rows.shape[0] // 2
    high, low = split(rows)
    by_real = dot3(high, low, right_high[0], right_low[0])
    by_imag = dot3(high, low, right_high[1], right_low[1])
    return by_real[:m] - by_imag[m:], by_imag[:m] + by_real[m:]


def kernel(n, order_ref, stem_ref, branch_ref, out_ref, stem, xh, xl, bh, bl, dh, dl, wh, wl,
           lch, lcl, sent, got, acc, load_sem, branch_sem, out_sem, send_sem, recv_sem, *branch):
    bw = stem.shape[1]
    rows = bw // n
    per = LANES // rows
    groups = n // per
    me = lax.axis_index("mode")
    z, q = lax.div(me, per), lax.rem(me, per)
    sequence = [groups // 2] + [s for s in range(1, groups) if s != groups // 2] + [0]
    early = sequence[: groups // 2]

    def column(s):
        return pl.ds(pl.multiple_of(flip(z, s, groups) * LANES, LANES), LANES)

    stem_copy = pltpu.make_async_copy(stem_ref, stem, load_sem)
    stem_copy.start()
    branch_copies = {}
    for s in sequence:
        branch_copies[s] = pltpu.make_async_copy(branch_ref.at[:, :, :, column(s)], branch[s], branch_sem.at[s])
        branch_copies[s].start()

    barrier = pltpu.get_barrier_semaphore()
    for k in range(1, n):
        pl.semaphore_signal(barrier, inc=1, device_id={"mode": flip(me, k, n)}, device_id_type=MESH)
    o0, o1, o2, o3 = (order_ref[k] for k in range(4))

    def first_rows(s):
        left = jnp.concatenate([branch[s][o0, part].T for part in range(2)], axis=0)
        return complex_rows(left, xh, xl)

    def hop(s, k):
        j = flip(q, k, per)
        return pltpu.make_async_remote_copy(
            src_ref=sent.at[s, j], dst_ref=got.at[s, q], send_sem=send_sem.at[s, k], recv_sem=recv_sem.at[s, q],
            device_id={"mode": flip(z, s, groups) * per + j}, device_id_type=MESH)

    def own(s):
        return pltpu.make_async_copy(sent.at[s, q], got.at[s, q], recv_sem.at[s, q])

    def send(s, real, imag):
        for j in range(per):
            sent[s, j, 0] = real[j * rows:(j + 1) * rows]
            sent[s, j, 1] = imag[j * rows:(j + 1) * rows]
        for k in range(per):
            own(s).start() if s == 0 and k == 0 else hop(s, k).start()

    stem_copy.wait()
    for part in range(2):
        xh[part], xl[part] = split(stem[part])
    for index, s in enumerate(sequence[: len(early)]):
        branch_copies[s].wait()
        real, imag = first_rows(s)
        if index == 0:
            pl.semaphore_wait(barrier, n - 1)
        send(s, real, imag)
    for s in sequence[len(early):]:
        branch_copies[s].wait()

    for s in range(groups):
        for part in range(2):
            bh[part, :, column(s)], bl[part, :, column(s)] = split(branch[s][o1, part])
            dh[part, :, column(s)], dl[part, :, column(s)] = split(branch[s][o3, part])

    def both(i, carry):
        at = pl.ds(pl.multiple_of(i * LANES, LANES), LANES)
        high = jnp.concatenate([bh[0, at], bh[1, at]], axis=0)
        low = jnp.concatenate([bl[0, at], bl[1, at]], axis=0)
        by_real = dot3(high, low, dh[0], dl[0])
        by_imag = dot3(high, low, dh[1], dl[1])
        wh[0, at], wl[0, at] = split(by_real[:LANES] - by_imag[LANES:])
        wh[1, at], wl[1, at] = split(by_imag[:LANES] + by_real[LANES:])
        return carry

    lax.fori_loop(0, bw // LANES, both, 0)

    for s in sequence[len(early):]:
        real, imag = first_rows(s)
        send(s, *complex_rows(jnp.concatenate([real, imag], axis=0), wh, wl))

    for s in range(groups):
        for t in range(groups):
            real, imag = (split(branch[t][o2, part, column(s), :].T) for part in range(2))
            top = column(t)
            low_half = pl.ds(pl.multiple_of(bw + flip(z, t, groups) * LANES, LANES), LANES)
            for ref, r, i in ((lch, real[0], imag[0]), (lcl, real[1], imag[1])):
                ref[s, top, :LANES] = r
                ref[s, top, LANES:] = -i
                ref[s, low_half, :LANES] = i
                ref[s, low_half, LANES:] = r

    arrivals = [0] + [s for s in early if s != groups // 2] + [groups // 2] + [s for s in sequence[len(early):] if s]
    tile = 2 * LANES
    for index, s in enumerate(arrivals):
        for j in range(per):
            pltpu.make_async_copy(got.at[s, j], got.at[s, j], recv_sem.at[s, j]).wait()
        real = jnp.concatenate([got[s, j, 0] for j in range(per)], axis=0)
        imag = jnp.concatenate([got[s, j, 1] for j in range(per)], axis=0)
        arrived = jnp.concatenate([real, imag], axis=0)
        if s in early:
            arrived = jnp.concatenate(complex_rows(arrived, wh, wl), axis=0)
        right_high, right_low = split(arrived)
        for i in range(2 * bw // tile):
            at = slice(i * tile, (i + 1) * tile)
            add = dot3(lch[s, at], lcl[s, at], right_high, right_low)
            acc[at] = add if index == 0 else acc[at] + add
            if index == len(arrivals) - 1:
                part, row = divmod(i * tile, bw)
                pltpu.make_async_copy(acc.at[at], out_ref.at[part, pl.ds(row, tile)], out_sem.at[i]).start()
    for i in range(2 * bw // tile):
        part, row = divmod(i * tile, bw)
        pltpu.make_async_copy(acc.at[pl.ds(i * tile, tile)], out_ref.at[part, pl.ds(row, tile)], out_sem.at[i]).wait()
    for s in range(groups):
        for k in range(per):
            if s or k:
                hop(s, k).wait_send()


def fused(n, stem_tensor, branch_tensors, branch_order):
    bw = stem_tensor.shape[-1]
    rows = bw // n
    per = LANES // rows
    groups = n // per
    square = pltpu.VMEM((2, bw, bw), BF16)
    window = pltpu.VMEM((groups, 2 * bw, 2 * LANES), BF16)
    return pl.pallas_call(
        functools.partial(kernel, n),
        out_shape=jax.ShapeDtypeStruct((2, bw, bw), F32),
        in_specs=[pl.BlockSpec(memory_space=pltpu.SMEM)] + [pl.BlockSpec(memory_space=pl.ANY)] * 2,
        out_specs=pl.BlockSpec(memory_space=pl.ANY),
        scratch_shapes=[
            pltpu.VMEM((2, bw, bw), F32),
            *[square] * 8,
            window,
            window,
            pltpu.VMEM((groups, per, 2, rows, bw), F32),
            pltpu.VMEM((groups, per, 2, rows, bw), F32),
            pltpu.VMEM((2 * bw, bw), F32),
            pltpu.SemaphoreType.DMA,
            pltpu.SemaphoreType.DMA((groups,)),
            pltpu.SemaphoreType.DMA((bw // LANES,)),
            pltpu.SemaphoreType.DMA((groups, per)),
            pltpu.SemaphoreType.DMA((groups, per)),
            *[pltpu.VMEM((4, 2, bw, LANES), F32)] * groups,
        ],
        compiler_params=pltpu.CompilerParams(collective_id=0, has_side_effects=True, vmem_limit_bytes=56 << 20),
    )(branch_order, stem_tensor.reshape(2, bw, bw), branch_tensors).reshape(stem_tensor.shape)


def complex_product(first, second, form):
    high = lax.Precision.HIGHEST
    real = jnp.einsum(form, first[0], second[0], precision=high) - jnp.einsum(form, first[1], second[1], precision=high)
    imag = jnp.einsum(form, first[0], second[1], precision=high) + jnp.einsum(form, first[1], second[0], precision=high)
    return jnp.stack([real, imag])


def plain(stem_tensor, branch_tensors, branch_order):
    field = stem_tensor[:, :, 0]
    chosen = [branch_tensors[branch_order[index]] for index in range(4)]
    field = complex_product(field, chosen[0], "sce,cd->sde")
    field = complex_product(field, chosen[1], "sce,ed->scd")
    moved = lax.all_to_all(field[:, :, None], "mode", split_axis=3, concat_axis=2, tiled=True)
    merged = moved.reshape(field.shape)
    merged = complex_product(merged, chosen[2], "sce,cd->sde")
    return complex_product(merged, chosen[3], "sce,ed->scd")[:, :, None]


def on_device(n, stem_tensor, branch_tensors, branch_order):
    _, stems, held, bw, _ = stem_tensor.shape
    rows = bw // n
    fits = stems == held == 1 and rows % 8 == 0 and rows < LANES and n & (n - 1) == 0 and n * rows == bw
    if fits and bw % (2 * LANES) == 0:
        return fused(n, stem_tensor, branch_tensors, branch_order)
    return plain(stem_tensor, branch_tensors, branch_order)


def solution(mesh):
    return jax.shard_map(
        functools.partial(on_device, mesh.shape["mode"]),
        mesh=mesh,
        in_specs=(P(None, "cuts", "mode", None, None), P(), P()),
        out_specs=P(None, "cuts", "mode", None, None),
        check_vma=False,
    )
```

time: 114 us -> 59.2 us (0.52); the launches traced: 112 us -> 59 us
  Pallas kernels: 0 us -> 55.9 us
  matrix products: 47.4 us -> 0 us
  waiting for transfers between devices: 42.2 us -> 0 us
  between operations: 7.96 us -> 0.01 us
  starting transfers between devices: 6.58 us -> 0 us
  local copies, waits for them, and re-layouts: 6.03 us -> 3.08 us
  other arithmetic: 1.66 us -> 0 us
    pallas_call x0 -> x1, Pallas kernels: none -> 55.9 us  [fused(): pl.pallas_call(functools.partial(kernel, n), out_shape=jax.ShapeDtypeStru...]
    dot_general x16 -> x0, matrix products: 47.4 us -> none  [the longest x4 13.6 us: complex_product(): jnp.einsum(form, first[0], second[1], precision=high)]
    all_to_all x1 -> x0, waiting for transfers between devices: 42.2 us -> none  [on_device(): lax.all_to_all(field[:, :, None], 'mode', split_axis=3, concat_axis=2, ti...]
    all_to_all x1 -> x0, starting transfers between devices: 6.58 us -> none  [on_device(): lax.all_to_all(field[:, :, None], 'mode', split_axis=3, concat_axis=2, ti...]
    slice x2 -> x0, local copies, waits for them, and re-layouts: 3.07 us -> none  [the longest x1 1.62 us: complex_product(): first[1]]
    unnamed x6 -> x1, local copies, waits for them, and re-layouts: 0.02 us -> 3.08 us
    broadcast_in_dim x1 -> x0, local copies, waits for them, and re-layouts: 2.94 us -> none  [on_device(): field[:, :, None]]
    broadcast_in_dim x2 -> x0, other arithmetic: 1.66 us -> none  [the longest x1 1.49 us: on_device(): return complex_product(merged, chosen[3], 'sce,ed->scd')[:, :, None]]
  transfers between devices with their start and end apart: 1 -> 0, of which waited for: 1 -> 0; matrix products, arithmetic and copies ran while one was open for 0% -> 0% of each run, Pallas kernels for 0% -> 0%
where the time goes in v1:
time: 59.2 us; the launch traced here: 59 us
  Pallas kernels  55.9 us (94%)
  local copies, waits for them, and re-layouts  3.08 us (5%)
    pallas_call x1, Pallas kernels, fused(): pl.pallas_call(functools.partial(kernel, n), out_shape=jax.ShapeDtypeStru...  55.9 us
    unnamed x1, local copies, waits for them, and re-layouts  3.08 us

profile of v1, /device:TPU:9, one launch (start us, length us, event | category | flops | bytes accessed | tf_op | source)
XLA Modules:
  0.0 59.0 jit_solution(2494723544470138725)
XLA Ops:
  0.0 55.9 %shard_map.37 = f32[2,512,512]{2,1,0:T(8,128)} custom-call(s32[4]{0:T(128)} %order_ref.1, f32[2,512,512]{2,1,0:T(8,128)} %bitcast.5, f32[4,2,512,512]{3,2,1,0:T(8,128)} %branch_ref.1), custom_call_target="tpu_custom_call" | custom-call | tf_op jit(solution)/shard_map/pallas_call | solution.py:169
  55.9 3.1 %copy.6 = f32[2,1,1,512,512]{4,3,2,1,0:T(8,128)} copy(f32[2,1,1,512,512]{4,3,2,1,0:T(8,128)} %bitcast.4) | data formatting | bytes 4194304

commit v2 on v1

--- a/solution.py
+++ b/solution.py
@@ -43,7 +43,7 @@
 
 
 def kernel(n, order_ref, stem_ref, branch_ref, out_ref, stem, xh, xl, bh, bl, dh, dl, wh, wl,
-           lch, lcl, sent, got, acc, load_sem, branch_sem, out_sem, send_sem, recv_sem, *branch):
+           lch, lcl, lct, sent, got, acc, load_sem, branch_sem, out_sem, send_sem, recv_sem, *branch):
     bw = stem.shape[1]
     rows = bw // n
     per = LANES // rows
@@ -56,21 +56,25 @@
     def column(s):
         return pl.ds(pl.multiple_of(flip(z, s, groups) * LANES, LANES), LANES)
 
-    stem_copy = pltpu.make_async_copy(stem_ref, stem, load_sem)
-    stem_copy.start()
+    stem_copies = [pltpu.make_async_copy(stem_ref.at[part], stem.at[part], load_sem.at[part]) for part in range(2)]
     branch_copies = {}
     for s in sequence:
         branch_copies[s] = pltpu.make_async_copy(branch_ref.at[:, :, :, column(s)], branch[s], branch_sem.at[s])
-        branch_copies[s].start()
+        if s == sequence[0]:
+            branch_copies[s].start()
+    for copy in stem_copies:
+        copy.start()
 
     barrier = pltpu.get_barrier_semaphore()
     for k in range(1, n):
         pl.semaphore_signal(barrier, inc=1, device_id={"mode": flip(me, k, n)}, device_id_type=MESH)
     o0, o1, o2, o3 = (order_ref[k] for k in range(4))
 
+    def left_rows(s):
+        return jnp.concatenate([branch[s][o0, part].T for part in range(2)], axis=0)
+
     def first_rows(s):
-        left = jnp.concatenate([branch[s][o0, part].T for part in range(2)], axis=0)
-        return complex_rows(left, xh, xl)
+        return complex_rows(left_rows(s), xh, xl)
 
     def hop(s, k):
         j = flip(q, k, per)
@@ -88,15 +92,22 @@
         for k in range(per):
             own(s).start() if s == 0 and k == 0 else hop(s, k).start()
 
-    stem_copy.wait()
+    branch_copies[sequence[0]].wait()
+    high, low = split(left_rows(sequence[0]))
+    by = []
     for part in range(2):
+        stem_copies[part].wait()
+        if part == 1:
+            for s in sequence[1:]:
+                branch_copies[s].start()
         xh[part], xl[part] = split(stem[part])
-    for index, s in enumerate(sequence[: len(early)]):
+        by.append(dot3(high, low, xh[part], xl[part]))
+    real, imag = by[0][:LANES] - by[1][LANES:], by[1][:LANES] + by[0][LANES:]
+    pl.semaphore_wait(barrier, n - 1)
+    send(sequence[0], real, imag)
+    for s in early[1:]:
         branch_copies[s].wait()
-        real, imag = first_rows(s)
-        if index == 0:
-            pl.semaphore_wait(barrier, n - 1)
-        send(s, real, imag)
+        send(s, *first_rows(s))
     for s in sequence[len(early):]:
         branch_copies[s].wait()
 
@@ -121,9 +132,19 @@
         real, imag = first_rows(s)
         send(s, *complex_rows(jnp.concatenate([real, imag], axis=0), wh, wl))
 
+    last = sequence[-2]
+
+    def third_rows(t, part, s):
+        if s != last:
+            return branch[t][o2, part, column(s), :]
+        base = flip(z, s, groups) * LANES
+        return jnp.concatenate([
+            branch[t][o2, part, pl.ds(pl.multiple_of(base + flip(q, k, per) * rows, rows), rows), :]
+            for k in range(per)], axis=0)
+
     for s in range(groups):
         for t in range(groups):
-            real, imag = (split(branch[t][o2, part, column(s), :].T) for part in range(2))
+            real, imag = (split(third_rows(t, part, s).T) for part in range(2))
             top = column(t)
             low_half = pl.ds(pl.multiple_of(bw + flip(z, t, groups) * LANES, LANES), LANES)
             for ref, r, i in ((lch, real[0], imag[0]), (lcl, real[1], imag[1])):
@@ -131,15 +152,30 @@
                 ref[s, top, LANES:] = -i
                 ref[s, low_half, :LANES] = i
                 ref[s, low_half, LANES:] = r
+            if s == last:
+                tail = slice(LANES - rows, LANES)
+                for place, (r, i) in enumerate(((real[0], imag[0]), (real[0], imag[0]), (real[1], imag[1]))):
+                    at = slice(2 * place * rows, (2 * place + 1) * rows)
+                    after = slice((2 * place + 1) * rows, (2 * place + 2) * rows)
+                    lct[top, at] = r[:, tail]
+                    lct[top, after] = -i[:, tail]
+                    lct[low_half, at] = i[:, tail]
+                    lct[low_half, after] = r[:, tail]
 
     arrivals = [0] + [s for s in early if s != groups // 2] + [groups // 2] + [s for s in sequence[len(early):] if s]
     tile = 2 * LANES
+
+    def arrive(s, j):
+        pltpu.make_async_copy(got.at[s, j], got.at[s, j], recv_sem.at[s, j]).wait()
+
     for index, s in enumerate(arrivals):
-        for j in range(per):
-            pltpu.make_async_copy(got.at[s, j], got.at[s, j], recv_sem.at[s, j]).wait()
-        real = jnp.concatenate([got[s, j, 0] for j in range(per)], axis=0)
-        imag = jnp.concatenate([got[s, j, 1] for j in range(per)], axis=0)
-        arrived = jnp.concatenate([real, imag], axis=0)
+        places = [flip(q, k, per) if s == last else k for k in range(per)]
+        if s == last:
+            final = places.pop()
+        for j in places:
+            arrive(s, j)
+        blank = [jnp.zeros((rows, bw), F32)] * (per - len(places))
+        arrived = jnp.concatenate([piece for part in range(2) for piece in [got[s, j, part] for j in places] + blank], axis=0)
         if s in early:
             arrived = jnp.concatenate(complex_rows(arrived, wh, wl), axis=0)
         right_high, right_low = split(arrived)
@@ -147,9 +183,14 @@
             at = slice(i * tile, (i + 1) * tile)
             add = dot3(lch[s, at], lcl[s, at], right_high, right_low)
             acc[at] = add if index == 0 else acc[at] + add
-            if index == len(arrivals) - 1:
-                part, row = divmod(i * tile, bw)
-                pltpu.make_async_copy(acc.at[at], out_ref.at[part, pl.ds(row, tile)], out_sem.at[i]).start()
+    arrive(last, final)
+    high, low = split(jnp.concatenate([got[last, final, 0], got[last, final, 1]], axis=0))
+    right = jnp.concatenate([high, low, high], axis=0)
+    for i in range(2 * bw // tile):
+        at = slice(i * tile, (i + 1) * tile)
+        acc[at] = acc[at] + dot(lct[at, : 6 * rows], right)
+        part, row = divmod(i * tile, bw)
+        pltpu.make_async_copy(acc.at[at], out_ref.at[part, pl.ds(row, tile)], out_sem.at[i]).start()
     for i in range(2 * bw // tile):
         part, row = divmod(i * tile, bw)
         pltpu.make_async_copy(acc.at[pl.ds(i * tile, tile)], out_ref.at[part, pl.ds(row, tile)], out_sem.at[i]).wait()
@@ -165,6 +206,7 @@
     per = LANES // rows
     groups = n // per
     square = pltpu.VMEM((2, bw, bw), BF16)
+    hbm = functools.partial(pltpu.with_memory_space_constraint, memory_space=pltpu.HBM)
     window = pltpu.VMEM((groups, 2 * bw, 2 * LANES), BF16)
     return pl.pallas_call(
         functools.partial(kernel, n),
@@ -176,18 +218,19 @@
             *[square] * 8,
             window,
             window,
+            pltpu.VMEM((2 * bw, 2 * LANES), BF16),
             pltpu.VMEM((groups, per, 2, rows, bw), F32),
             pltpu.VMEM((groups, per, 2, rows, bw), F32),
             pltpu.VMEM((2 * bw, bw), F32),
-            pltpu.SemaphoreType.DMA,
+            pltpu.SemaphoreType.DMA((2,)),
             pltpu.SemaphoreType.DMA((groups,)),
             pltpu.SemaphoreType.DMA((bw // LANES,)),
             pltpu.SemaphoreType.DMA((groups, per)),
             pltpu.SemaphoreType.DMA((groups, per)),
             *[pltpu.VMEM((4, 2, bw, LANES), F32)] * groups,
         ],
-        compiler_params=pltpu.CompilerParams(collective_id=0, has_side_effects=True, vmem_limit_bytes=56 << 20),
-    )(branch_order, stem_tensor.reshape(2, bw, bw), branch_tensors).reshape(stem_tensor.shape)
+        compiler_params=pltpu.CompilerParams(collective_id=0, has_side_effects=True, vmem_limit_bytes=32 << 20),
+    )(hbm(branch_order), hbm(stem_tensor.reshape(2, bw, bw)), hbm(branch_tensors)).reshape(stem_tensor.shape)
 
 
 def complex_product(first, second, form):
@@ -211,8 +254,8 @@
 def on_device(n, stem_tensor, branch_tensors, branch_order):
     _, stems, held, bw, _ = stem_tensor.shape
     rows = bw // n
-    fits = stems == held == 1 and rows % 8 == 0 and rows < LANES and n & (n - 1) == 0 and n * rows == bw
-    if fits and bw % (2 * LANES) == 0:
+    fits = stems == held == 1 and rows % 8 == 0 and 3 * rows <= LANES and n & (n - 1) == 0 and n * rows == bw
+    if fits and bw % (4 * LANES) == 0:
         return fused(n, stem_tensor, branch_tensors, branch_order)
     return plain(stem_tensor, branch_tensors, branch_order)
 

time: 59.2 us -> 55.1 us (0.931)
  Pallas kernels: 55.9 us -> 53.7 us
  local copies, waits for them, and re-layouts: 3.08 us -> 1.32 us
    pallas_call x1, Pallas kernels: 55.9 us -> 53.7 us  [fused(): pl.pallas_call(functools.partial(kernel, n), out_shape=jax.ShapeDtypeStru...]
    unnamed x1, local copies, waits for them, and re-layouts: 3.08 us -> 1.32 us
where the time goes in v2:
time: 55.1 us; the launch traced here: 55 us
  Pallas kernels  53.7 us (97%)
  local copies, waits for them, and re-layouts  1.32 us (2%)
    pallas_call x1, Pallas kernels, fused(): pl.pallas_call(functools.partial(kernel, n), out_shape=jax.ShapeDtypeStru...  53.7 us
    unnamed x1, local copies, waits for them, and re-layouts  1.32 us

profile of v2, /device:TPU:9, one launch (start us, length us, event | category | flops | bytes accessed | tf_op | source)
XLA Modules:
  0.0 55.0 jit_solution(16361204420117940919)
XLA Ops:
  0.0 53.7 %shard_map.37 = f32[2,512,512]{2,1,0:T(8,128)S(1)} custom-call(s32[4]{0:T(128)} %order_ref.1, f32[2,512,512]{2,1,0:T(8,128)} %bitcast.5, f32[4,2,512,512]{3,2,1,0:T(8,128)} %branch_ref.1), custom_call_target="tpu_custom_call" | custom-call | tf_op jit(solution)/shard_map/pallas_call | solution.py:211
  53.7 1.3 %copy.6 = f32[2,1,1,512,512]{4,3,2,1,0:T(8,128)} copy(f32[2,1,1,512,512]{4,3,2,1,0:T(8,128)S(1)} %bitcast.4) | data formatting | bytes 4194304
